TPU v7x, 32 devices: a whole 2x2x4 slice. The times are simulated.
32 devices in a mesh: seq: 16 (over z, y, x), head: 2 (over core).
Axes of the slice: x: 2, y: 2, z: 4, core: 2. Of those that a mesh axis runs over, the one named last changes fastest.
Arguments:
- attn_q: bfloat16 [2048, 512], P('seq', 'head'), may hold values from -6 to 6
- attn_k: bfloat16 [2048, 512], P('seq', 'head'), may hold values from -6 to 6
- attn_v: bfloat16 [2048, 512], P('seq', 'head'), may hold values from -6 to 6
- attn_out: bfloat16 [2048, 512], P('seq', 'head'), may hold values from -0.29882812 to 0.29882812
- attn_dout: bfloat16 [2048, 512], P('seq', 'head'), may hold values from -96 to 96
- attn_lse: float32 [4, 2048], P('head', 'seq'), may hold values from 7 to 8
- w_kv: bfloat16 [512, 2, 512], P('seq', None, 'head'), may hold values from -0.25 to 0.25
- gdn_q: bfloat16 [2048, 512], P('seq', 'head'), may hold values from -6 to 6
- gdn_k: bfloat16 [2048, 512], P('seq', 'head'), may hold values from -6 to 6
- gdn_v: bfloat16 [2048, 512], P('seq', 'head'), may hold values from -6 to 6
- gdn_dout: bfloat16 [2048, 512], P('seq', 'head'), may hold values from -6 to 6
- gdn_log_decay: float32 [4, 2048], P('head', 'seq'), may hold values from -0.56 to 0
- gdn_beta: float32 [4, 2048], P('head', 'seq'), may hold values from 0 to 0.9
- gdn_states: float32 [32, 4, 128, 128], P('seq', 'head'), may hold values from -24 to 24
Outputs:
- attn_dq: bfloat16 [2048, 512], P('seq', 'head')
- attn_dx: bfloat16 [512, 2048], P('head', 'seq')
- gdn_dq: bfloat16 [2048, 512], P('seq', 'head')
- gdn_dk: bfloat16 [2048, 512], P('seq', 'head')
- gdn_dv: bfloat16 [2048, 512], P('seq', 'head')
- gdn_dlog_decay: float32 [4, 2048], P('head', 'seq')
- gdn_dbeta: float32 [4, 2048], P('head', 'seq')
All inputs are finite; a program needn't handle non-finite values.
Results may differ from a plain program's by a relative error of at most 0.0078.
Values may be sent and summed in bfloat16 or wider, within the bound.
A program may use at most 64 MiB of HBM per device.

v0:
```python
import jax
import jax.numpy as jnp
from jax import lax
from jax.sharding import PartitionSpec as P

BLOCK = 64
WINDOW = 1024
HIGH = lax.Precision.HIGHEST


def from_behind(block, axis, distance):
    devices = range(lax.axis_size(axis))
    route = [(i - distance, i) for i in devices if i - distance in devices]
    return lax.ppermute(block, axis, route)


def matmul(left_side, right_side):
    return jnp.dot(left_side, right_side, precision=HIGH)


def stack_mul(left_side, right_side):
    return jnp.einsum("hij,hjk->hik", left_side, right_side, precision=HIGH)


def unit_rows(matrix):
    return matrix * lax.rsqrt(jnp.sum(matrix * matrix, axis=-1, keepdims=True) + 1e-06)


def inverse_unit(lower_part):
    length = lower_part.shape[0]
    identity = jnp.eye(length, dtype=jnp.float32)
    powered = lower_part
    result = identity - lower_part
    for _ in range(length.bit_length() - 2):
        powered = matmul(powered, powered)
        result = matmul(result, identity + powered)
    return result


def block_parts(queries, keys_in, decays, strengths):
    length, depth = queries.shape
    unit_q = unit_rows(queries) * depth ** (-0.5)
    unit_k = unit_rows(keys_in)
    summed = jnp.cumsum(decays)
    row_ids = lax.broadcasted_iota(jnp.int32, (length, length), 0)
    col_ids = lax.broadcasted_iota(jnp.int32, (length, length), 1)
    causal = row_ids >= col_ids
    fading = jnp.where(
        causal, jnp.exp(jnp.where(causal, summed[:, None] - summed[None, :], 0.0)), 0.0
    )
    strict = jnp.where(row_ids > col_ids, fading, 0.0)
    lower_part = strengths[:, None] * strict * matmul(unit_k, unit_k.T)
    solved = inverse_unit(lower_part)
    growth = jnp.exp(summed)
    widened = matmul(solved, (strengths * growth)[:, None] * unit_k)
    attention = fading * matmul(unit_q, unit_k.T)
    tailing = jnp.exp(summed[-1] - summed)[:, None] * unit_k
    return (unit_q, solved, growth, widened, attention, tailing)


def block_forward(queries, keys_in, values, decays, strengths, initial):
    unit_q, solved, growth, widened, attention, tailing = block_parts(
        queries, keys_in, decays, strengths
    )
    fresh = matmul(solved, strengths[:, None] * values) - matmul(widened, initial)
    output = growth[:, None] * matmul(unit_q, initial) + matmul(attention, fresh)
    final = growth[-1] * initial + matmul(tailing.T, fresh)
    return (output, final)


def block_adjoint(queries, keys_in, decays, strengths, out_grad):
    unit_q, solved, growth, widened, attention, tailing = block_parts(
        queries, keys_in, decays, strengths
    )
    depth = queries.shape[1]
    carry_map = growth[-1] * jnp.eye(depth, dtype=jnp.float32) - matmul(widened.T, tailing)
    local_term = matmul((growth[:, None] * unit_q).T, out_grad) - matmul(
        widened.T, matmul(attention.T, out_grad)
    )
    return (carry_map, local_term)


def block_grads(queries, keys_in, values, decays, strengths, initial, out_grad, later_adjoint):
    _, pullback = jax.vjp(block_forward, queries, keys_in, values, decays, strengths, initial)
    grad_q, grad_k, grad_v, grad_decay, grad_beta, _ = pullback((out_grad, later_adjoint))
    return (grad_q, grad_k, grad_v, grad_decay, grad_beta)


def window_terms(queries, keys_in, values, out_grad, log_totals, dot_terms, query_pos, key_pos):
    scaling = queries.shape[2] ** (-0.5)
    logits = (
        jnp.einsum("rhd,khd->hrk", queries, keys_in, preferred_element_type=jnp.float32) * scaling
    )
    distance = query_pos[:, None] - key_pos[None, :]
    visible = ((distance >= 0) & (distance < WINDOW) & (key_pos[None, :] >= 0))[None, :, :]
    chances = jnp.where(
        visible, jnp.exp(jnp.where(visible, logits - log_totals[:, :, None], 0.0)), 0.0
    )
    grad_prob = jnp.einsum("rhd,khd->hrk", out_grad, values, preferred_element_type=jnp.float32)
    grad_logit = (chances * (grad_prob - dot_terms[:, :, None])).astype(jnp.bfloat16)
    weights = chances.astype(jnp.bfloat16)
    grad_q = (
        jnp.einsum("hrk,khd->rhd", grad_logit, keys_in, preferred_element_type=jnp.float32)
        * scaling
    )
    grad_k = (
        jnp.einsum("hrk,rhd->khd", grad_logit, queries, preferred_element_type=jnp.float32)
        * scaling
    )
    grad_v = jnp.einsum("hrk,rhd->khd", weights, out_grad, preferred_element_type=jnp.float32)
    return (grad_q, grad_k, grad_v)


def per_device(
    attn_q,
    attn_k,
    attn_v,
    attn_out,
    attn_dout,
    attn_lse,
    w_kv,
    gdn_q,
    gdn_k,
    gdn_v,
    gdn_dout,
    gdn_log_decay,
    gdn_beta,
    gdn_states,
):
    row_count, column_count = attn_q.shape
    head_count = attn_lse.shape[0]
    depth = column_count // head_count
    reach_count = WINDOW // row_count
    position = lax.axis_index("seq")

    def by_heads(matrix):
        return matrix.reshape(-1, head_count, depth)

    dot_terms = jnp.sum(
        by_heads(attn_dout).astype(jnp.float32) * by_heads(attn_out).astype(jnp.float32), axis=2
    ).T
    query_pos = position * row_count + jnp.arange(row_count, dtype=jnp.int32)
    couple = jnp.stack([attn_k, attn_v])
    pieces = []
    for offset_by in range(reach_count, 0, -1):
        pieces.append(from_behind(couple, "seq", offset_by))
    before = jnp.concatenate(pieces, axis=1)
    window = jnp.concatenate([before, couple], axis=1)
    key_pos = (position - reach_count) * row_count + jnp.arange(
        (reach_count + 1) * row_count, dtype=jnp.int32
    )
    grad_q, grad_k, grad_v = window_terms(
        by_heads(attn_q),
        by_heads(window[0]),
        by_heads(window[1]),
        by_heads(attn_dout),
        attn_lse,
        dot_terms,
        query_pos,
        key_pos,
    )
    own_rows = jnp.stack([attn_q, attn_dout])
    own_stats = jnp.stack([attn_lse, dot_terms])
    query_parts = [own_rows]
    stat_parts = [own_stats]
    for offset_by in range(1, reach_count + 1):
        query_parts.append(from_behind(own_rows, "seq", -offset_by))
        stat_parts.append(from_behind(own_stats, "seq", -offset_by))
    later_rows = jnp.concatenate(query_parts, axis=1)
    later_stats = jnp.concatenate(stat_parts, axis=2)
    later_pos = position * row_count + jnp.arange((reach_count + 1) * row_count, dtype=jnp.int32)
    _, own_k, own_v = window_terms(
        by_heads(later_rows[0]),
        by_heads(attn_k),
        by_heads(attn_v),
        by_heads(later_rows[1]),
        later_stats[0],
        later_stats[1],
        later_pos,
        query_pos,
    )
    key_grad = own_k.reshape(row_count, column_count).astype(jnp.bfloat16)
    value_grad = own_v.reshape(row_count, column_count).astype(jnp.bfloat16)
    attn_dq = grad_q.reshape(row_count, column_count).astype(jnp.bfloat16)
    row_piece = lax.all_gather(w_kv, "seq", axis=0, tiled=True)
    from_keys = lax.dot_general(
        row_piece[:, 0, :], key_grad, (((1,), (1,)), ((), ())), preferred_element_type=jnp.float32
    )
    partial_value = from_keys + lax.dot_general(
        row_piece[:, 1, :], value_grad, (((1,), (1,)), ((), ())), preferred_element_type=jnp.float32
    )
    attn_dx = lax.psum_scatter(partial_value, "head", scatter_dimension=0, tiled=True).astype(
        jnp.bfloat16
    )
    block_count = row_count // BLOCK

    def by_blocks(matrix):
        return (
            matrix.reshape(block_count, BLOCK, head_count, depth)
            .transpose(0, 2, 1, 3)
            .astype(jnp.float32)
        )

    def gates_by_blocks(matrix):
        return matrix.reshape(head_count, block_count, BLOCK).transpose(1, 0, 2)

    queries = by_blocks(gdn_q)
    keys_in = by_blocks(gdn_k)
    values = by_blocks(gdn_v)
    out_grad = by_blocks(gdn_dout)
    decays = gates_by_blocks(gdn_log_decay)
    strengths = gates_by_blocks(gdn_beta)
    carry_map, local_term = jax.vmap(jax.vmap(block_adjoint))(
        queries, keys_in, decays, strengths, out_grad
    )
    identity = jnp.broadcast_to(jnp.eye(depth, dtype=jnp.float32), (head_count, depth, depth))
    nothing = jnp.zeros((head_count, depth, depth), jnp.float32)

    def compose_blocks(carry, couple_in):
        across, offset = carry
        return (
            (stack_mul(couple_in[0], across), stack_mul(couple_in[0], offset) + couple_in[1]),
            None,
        )

    (across, offset), _ = lax.scan(
        compose_blocks, (identity, nothing), (carry_map, local_term), reverse=True
    )

    def relay_step(step_no, incoming):
        return from_behind(stack_mul(across, incoming) + offset, "seq", -1)

    carried = lax.fori_loop(0, lax.axis_size("seq") - 1, relay_step, nothing)

    def backward(carry, couple_in):
        return (stack_mul(couple_in[0], carry) + couple_in[1], carry)

    _, later_adjoint = lax.scan(backward, carried, (carry_map, local_term), reverse=True)
    grad_bq, grad_bk, grad_bv, grad_decay, grad_beta = jax.vmap(jax.vmap(block_grads))(
        queries, keys_in, values, decays, strengths, gdn_states, out_grad, later_adjoint
    )

    def tokens_back(stacked):
        return stacked.transpose(0, 2, 1, 3).reshape(row_count, column_count).astype(jnp.bfloat16)

    def per_head(stacked):
        return stacked.transpose(1, 0, 2).reshape(head_count, row_count)

    return (
        attn_dq,
        attn_dx,
        tokens_back(grad_bq),
        tokens_back(grad_bk),
        tokens_back(grad_bv),
        per_head(grad_decay),
        per_head(grad_beta),
    )


def solution(mesh):
    placed = (
        P("seq", "head"),
        P("seq", "head"),
        P("seq", "head"),
        P("seq", "head"),
        P("seq", "head"),
        P("head", "seq"),
        P("seq", None, "head"),
        P("seq", "head"),
        P("seq", "head"),
        P("seq", "head"),
        P("seq", "head"),
        P("head", "seq"),
        P("head", "seq"),
        P("seq", "head", None, None),
    )
    return jax.shard_map(
        per_device,
        mesh=mesh,
        in_specs=placed,
        out_specs=(
            P("seq", "head"),
            P("head", "seq"),
            P("seq", "head"),
            P("seq", "head"),
            P("seq", "head"),
            P("head", "seq"),
            P("head", "seq"),
        ),
        check_vma=False,
    )
```

profile of v0, /device:TPU:0, one launch (start us, length us, event | category | flops | bytes accessed | tf_op | source)
XLA Modules:
  0.0 311.4 jit_solution(4315394593394781818)
XLA Ops:
  25.4 1.3 fusion.50
  30.9 133.4 %while.43 = (s32[]{:T(128)}, f32[2,128,128]{2,1,0:T(8,128)S(1)}, f32[2,128,128]{2,1,0:T(8,128)S(1)}, f32[2,128,128]{2,1,0:T(8,128)S(1)}, s32[]{:T(128)}) while((s32[]{:T(128)}, f32[2,128,128]{2,1,0:T(8,128)S(1)}, f32[2,128,128]{2,1,0:T(8,128)S(1)}, f32[2,128,128]{2,1,0:T(8,128)S(1)}, s32[]{:T(128)}) %tuple.116), condition=%wide.region_9.10_spmd, body=%wide.region_8.9_spmd.sunk | while | flops 50364416 | bytes 1048677 | solution.py:233
  32.5 7.7 %collective-permute-done = f32[2,128,128]{2,1,0:T(8,128)S(1)} collective-permute-done((f32[2,128,128]{2,1,0:T(8,128)S(1)}, f32[2,128,128]{2,1,0:T(8,128)S(1)}, u32[]{:S(2)}, u32[]{:S(2)}) %collective-permute-start) | collective-permute-done | bytes 131104 | tf_op jit(solution)/shard_map/while/body/eval_jaxpr/ppermute | solution.py:14
  41.8 6.8 %collective-permute-done = f32[2,128,128]{2,1,0:T(8,128)S(1)} collective-permute-done((f32[2,128,128]{2,1,0:T(8,128)S(1)}, f32[2,128,128]{2,1,0:T(8,128)S(1)}, u32[]{:S(2)}, u32[]{:S(2)}) %collective-permute-start) | collective-permute-done | bytes 131104 | tf_op jit(solution)/shard_map/while/body/eval_jaxpr/ppermute | solution.py:14
  48.8 1.3 collective-permute-start
  50.1 6.5 %collective-permute-done = f32[2,128,128]{2,1,0:T(8,128)S(1)} collective-permute-done((f32[2,128,128]{2,1,0:T(8,128)S(1)}, f32[2,128,128]{2,1,0:T(8,128)S(1)}, u32[]{:S(2)}, u32[]{:S(2)}) %collective-permute-start) | collective-permute-done | bytes 131104 | tf_op jit(solution)/shard_map/while/body/eval_jaxpr/ppermute | solution.py:14
  58.2 6.5 %collective-permute-done = f32[2,128,128]{2,1,0:T(8,128)S(1)} collective-permute-done((f32[2,128,128]{2,1,0:T(8,128)S(1)}, f32[2,128,128]{2,1,0:T(8,128)S(1)}, u32[]{:S(2)}, u32[]{:S(2)}) %collective-permute-start) | collective-permute-done | bytes 131104 | tf_op jit(solution)/shard_map/while/body/eval_jaxpr/ppermute | solution.py:14
  66.2 6.9 %collective-permute-done = f32[2,128,128]{2,1,0:T(8,128)S(1)} collective-permute-done((f32[2,128,128]{2,1,0:T(8,128)S(1)}, f32[2,128,128]{2,1,0:T(8,128)S(1)}, u32[]{:S(2)}, u32[]{:S(2)}) %collective-permute-start) | collective-permute-done | bytes 131104 | tf_op jit(solution)/shard_map/while/body/eval_jaxpr/ppermute | solution.py:14
  74.7 7.4 %collective-permute-done = f32[2,128,128]{2,1,0:T(8,128)S(1)} collective-permute-done((f32[2,128,128]{2,1,0:T(8,128)S(1)}, f32[2,128,128]{2,1,0:T(8,128)S(1)}, u32[]{:S(2)}, u32[]{:S(2)}) %collective-permute-start) | collective-permute-done | bytes 131104 | tf_op jit(solution)/shard_map/while/body/eval_jaxpr/ppermute | solution.py:14
  83.6 8.7 %collective-permute-done = f32[2,128,128]{2,1,0:T(8,128)S(1)} collective-permute-done((f32[2,128,128]{2,1,0:T(8,128)S(1)}, f32[2,128,128]{2,1,0:T(8,128)S(1)}, u32[]{:S(2)}, u32[]{:S(2)}) %collective-permute-start) | collective-permute-done | bytes 131104 | tf_op jit(solution)/shard_map/while/body/eval_jaxpr/ppermute | solution.py:14
  93.8 8.7 %collective-permute-done = f32[2,128,128]{2,1,0:T(8,128)S(1)} collective-permute-done((f32[2,128,128]{2,1,0:T(8,128)S(1)}, f32[2,128,128]{2,1,0:T(8,128)S(1)}, u32[]{:S(2)}, u32[]{:S(2)}) %collective-permute-start) | collective-permute-done | bytes 131104 | tf_op jit(solution)/shard_map/while/body/eval_jaxpr/ppermute | solution.py:14
  104.2 7.2 %collective-permute-done = f32[2,128,128]{2,1,0:T(8,128)S(1)} collective-permute-done((f32[2,128,128]{2,1,0:T(8,128)S(1)}, f32[2,128,128]{2,1,0:T(8,128)S(1)}, u32[]{:S(2)}, u32[]{:S(2)}) %collective-permute-start) | collective-permute-done | bytes 131104 | tf_op jit(solution)/shard_map/while/body/eval_jaxpr/ppermute | solution.py:14
  112.9 6.8 %collective-permute-done = f32[2,128,128]{2,1,0:T(8,128)S(1)} collective-permute-done((f32[2,128,128]{2,1,0:T(8,128)S(1)}, f32[2,128,128]{2,1,0:T(8,128)S(1)}, u32[]{:S(2)}, u32[]{:S(2)}) %collective-permute-start) | collective-permute-done | bytes 131104 | tf_op jit(solution)/shard_map/while/body/eval_jaxpr/ppermute | solution.py:14
  121.3 7.1 %collective-permute-done = f32[2,128,128]{2,1,0:T(8,128)S(1)} collective-permute-done((f32[2,128,128]{2,1,0:T(8,128)S(1)}, f32[2,128,128]{2,1,0:T(8,128)S(1)}, u32[]{:S(2)}, u32[]{:S(2)}) %collective-permute-start) | collective-permute-done | bytes 131104 | tf_op jit(solution)/shard_map/while/body/eval_jaxpr/ppermute | solution.py:14
  130.0 7.4 %collective-permute-done = f32[2,128,128]{2,1,0:T(8,128)S(1)} collective-permute-done((f32[2,128,128]{2,1,0:T(8,128)S(1)}, f32[2,128,128]{2,1,0:T(8,128)S(1)}, u32[]{:S(2)}, u32[]{:S(2)}) %collective-permute-start) | collective-permute-done | bytes 131104 | tf_op jit(solution)/shard_map/while/body/eval_jaxpr/ppermute | solution.py:14
  138.9 7.4 %collective-permute-done = f32[2,128,128]{2,1,0:T(8,128)S(1)} collective-permute-done((f32[2,128,128]{2,1,0:T(8,128)S(1)}, f32[2,128,128]{2,1,0:T(8,128)S(1)}, u32[]{:S(2)}, u32[]{:S(2)}) %collective-permute-start) | collective-permute-done | bytes 131104 | tf_op jit(solution)/shard_map/while/body/eval_jaxpr/ppermute | solution.py:14
  147.8 7.4 %collective-permute-done = f32[2,128,128]{2,1,0:T(8,128)S(1)} collective-permute-done((f32[2,128,128]{2,1,0:T(8,128)S(1)}, f32[2,128,128]{2,1,0:T(8,128)S(1)}, u32[]{:S(2)}, u32[]{:S(2)}) %collective-permute-start) | collective-permute-done | bytes 131104 | tf_op jit(solution)/shard_map/while/body/eval_jaxpr/ppermute | solution.py:14
  156.8 7.5 %collective-permute-done = f32[2,128,128]{2,1,0:T(8,128)S(1)} collective-permute-done((f32[2,128,128]{2,1,0:T(8,128)S(1)}, f32[2,128,128]{2,1,0:T(8,128)S(1)}, u32[]{:S(2)}, u32[]{:S(2)}) %collective-permute-start) | collective-permute-done | bytes 131104 | tf_op jit(solution)/shard_map/while/body/eval_jaxpr/ppermute | solution.py:14
  164.3 1.5 collective-permute-start.21
  180.5 54.2 %all_gather.3 = bf16[512,2,256]{2,0,1:T(8,128)(2,1)S(1)} all-gather(bf16[32,2,256]{2,0,1:T(8,128)(2,1)S(1)} %copy.284), channel_id=1, replica_groups=mesh['seq'=16,'head'=2] {'seq'}, dimensions={0}, use_global_device_ids=true | all-gather | bytes 557056 | tf_op jit(solution)/shard_map/all_gather | solution.py:185
  236.6 1.4 fusion.41
  242.9 1.3 collective-permute-start.22
  244.3 1.5 collective-permute-start.23
  257.5 1.9 collective-permute-done.11
  260.7 10.6 %collective-permute-start.1 = (bf16[2,128,256]{1,2,0:T(8,128)(2,1)S(1)}, bf16[2,128,256]{1,2,0:T(8,128)(2,1)}, u32[]{:S(2)}, u32[]{:S(2)}) collective-permute-start(bf16[2,128,256]{1,2,0:T(8,128)(2,1)S(1)} %pad_maximum_fusion), channel_id=1, source_target_pairs={{0,16},{2,18},{4,20},{6,22},{8,24},{10,26},{12,28},{14,30},{1,17},... | collective-permute-start | bytes 393224 | tf_op jit(solution)/shard_map/ppermute | solution.py:14
  271.3 6.4 %collective-permute-start.2 = (bf16[2,128,256]{1,2,0:T(8,128)(2,1)S(1)}, bf16[2,128,256]{1,2,0:T(8,128)(2,1)}, u32[]{:S(2)}, u32[]{:S(2)}) collective-permute-start(bf16[2,128,256]{1,2,0:T(8,128)(2,1)S(1)} %pad_maximum_fusion), channel_id=1, source_target_pairs={{0,14},{2,16},{4,18},{6,20},{8,22},{10,24},{12,26},{14,28},{16,30}... | collective-permute-start | bytes 393224 | tf_op jit(solution)/shard_map/ppermute | solution.py:14
  277.7 1.9 collective-permute-start.3
  279.7 2.0 collective-permute-start.4
  281.7 1.9 collective-permute-start.5
  287.8 3.0 collective-permute-start.6
  291.8 1.3 collective-permute-start.7
  294.0 3.1 collective-permute-start.8
  (307 shorter events, 93.0 us)
Async XLA Ops:
  7.2 295.8 %reduce-scatter.2.cloned.1.call-start = ((), (), s32[]{:S(2)}) async-start(), calls=%async_computation.1 | async-start | bytes 393216 | tf_op jit(solution)/shard_map/reduce_scatter | solution.py:192
  10.0 232.9 %collective-permute-start.17 = (f32[2,2,128]{2,1,0:T(2,128)S(1)}, f32[2,2,128]{2,1,0:T(2,128)S(1)}, u32[]{:S(2)}, u32[]{:S(2)}) collective-permute-start(f32[2,2,128]{2,1,0:T(2,128)S(1)} %get-tuple-element.350), channel_id=1, source_target_pairs={{2,0},{4,2},{6,4},{8,6},{10,8},{12,10},{14,12},{16,14},{18,16},{20... | collective-permute-start | bytes 6152 | tf_op jit(solution)/shard_map/ppermute | solution.py:14
  11.3 233.0 %collective-permute-start.18 = (f32[2,2,128]{2,1,0:T(2,128)S(1)}, f32[2,2,128]{2,1,0:T(2,128)S(1)}, u32[]{:S(2)}, u32[]{:S(2)}) collective-permute-start(f32[2,2,128]{2,1,0:T(2,128)S(1)} %get-tuple-element.350), channel_id=1, source_target_pairs={{4,0},{6,2},{8,4},{10,6},{12,8},{14,10},{16,12},{18,14},{20,16},{2... | collective-permute-start | bytes 6152 | tf_op jit(solution)/shard_map/ppermute | solution.py:14
  12.6 233.2 %collective-permute-start.19 = (f32[2,2,128]{2,1,0:T(2,128)S(1)}, f32[2,2,128]{2,1,0:T(2,128)S(1)}, u32[]{:S(2)}, u32[]{:S(2)}) collective-permute-start(f32[2,2,128]{2,1,0:T(2,128)S(1)} %get-tuple-element.350), channel_id=1, source_target_pairs={{6,0},{8,2},{10,4},{12,6},{14,8},{16,10},{18,12},{20,14},{22,16},{... | collective-permute-start | bytes 6152 | tf_op jit(solution)/shard_map/ppermute | solution.py:14
  13.9 233.2 %collective-permute-start.20 = (f32[2,2,128]{2,1,0:T(2,128)S(1)}, f32[2,2,128]{2,1,0:T(2,128)S(1)}, u32[]{:S(2)}, u32[]{:S(2)}) collective-permute-start(f32[2,2,128]{2,1,0:T(2,128)S(1)} %get-tuple-element.350), channel_id=1, source_target_pairs={{8,0},{10,2},{12,4},{14,6},{16,8},{18,10},{20,12},{22,14},{24,16},... | collective-permute-start | bytes 6152 | tf_op jit(solution)/shard_map/ppermute | solution.py:14
  31.2 9.0 %collective-permute-start = (f32[2,128,128]{2,1,0:T(8,128)S(1)}, f32[2,128,128]{2,1,0:T(8,128)S(1)}, u32[]{:S(2)}, u32[]{:S(2)}) collective-permute-start(f32[2,128,128]{2,1,0:T(8,128)S(1)} %convolution_add_fusion.20), channel_id=1, source_target_pairs={{2,0},{4,2},{6,4},{8,6},{10,8},{12,10},{14,12},{16,14},{18,16},{20... | collective-permute-start | bytes 393224 | tf_op jit(solution)/shard_map/while/body/eval_jaxpr/ppermute | solution.py:14
  40.4 8.1 %collective-permute-start = (f32[2,128,128]{2,1,0:T(8,128)S(1)}, f32[2,128,128]{2,1,0:T(8,128)S(1)}, u32[]{:S(2)}, u32[]{:S(2)}) collective-permute-start(f32[2,128,128]{2,1,0:T(8,128)S(1)} %convolution_add_fusion.20), channel_id=1, source_target_pairs={{2,0},{4,2},{6,4},{8,6},{10,8},{12,10},{14,12},{16,14},{18,16},{20... | collective-permute-start | bytes 393224 | tf_op jit(solution)/shard_map/while/body/eval_jaxpr/ppermute | solution.py:14
  64.9 8.2 %collective-permute-start = (f32[2,128,128]{2,1,0:T(8,128)S(1)}, f32[2,128,128]{2,1,0:T(8,128)S(1)}, u32[]{:S(2)}, u32[]{:S(2)}) collective-permute-start(f32[2,128,128]{2,1,0:T(8,128)S(1)} %convolution_add_fusion.20), channel_id=1, source_target_pairs={{2,0},{4,2},{6,4},{8,6},{10,8},{12,10},{14,12},{16,14},{18,16},{20... | collective-permute-start | bytes 393224 | tf_op jit(solution)/shard_map/while/body/eval_jaxpr/ppermute | solution.py:14
  73.4 8.7 %collective-permute-start = (f32[2,128,128]{2,1,0:T(8,128)S(1)}, f32[2,128,128]{2,1,0:T(8,128)S(1)}, u32[]{:S(2)}, u32[]{:S(2)}) collective-permute-start(f32[2,128,128]{2,1,0:T(8,128)S(1)} %convolution_add_fusion.20), channel_id=1, source_target_pairs={{2,0},{4,2},{6,4},{8,6},{10,8},{12,10},{14,12},{16,14},{18,16},{20... | collective-permute-start | bytes 393224 | tf_op jit(solution)/shard_map/while/body/eval_jaxpr/ppermute | solution.py:14
  82.3 10.0 %collective-permute-start = (f32[2,128,128]{2,1,0:T(8,128)S(1)}, f32[2,128,128]{2,1,0:T(8,128)S(1)}, u32[]{:S(2)}, u32[]{:S(2)}) collective-permute-start(f32[2,128,128]{2,1,0:T(8,128)S(1)} %convolution_add_fusion.20), channel_id=1, source_target_pairs={{2,0},{4,2},{6,4},{8,6},{10,8},{12,10},{14,12},{16,14},{18,16},{20... | collective-permute-start | bytes 393224 | tf_op jit(solution)/shard_map/while/body/eval_jaxpr/ppermute | solution.py:14
  92.5 10.0 %collective-permute-start = (f32[2,128,128]{2,1,0:T(8,128)S(1)}, f32[2,128,128]{2,1,0:T(8,128)S(1)}, u32[]{:S(2)}, u32[]{:S(2)}) collective-permute-start(f32[2,128,128]{2,1,0:T(8,128)S(1)} %convolution_add_fusion.20), channel_id=1, source_target_pairs={{2,0},{4,2},{6,4},{8,6},{10,8},{12,10},{14,12},{16,14},{18,16},{20... | collective-permute-start | bytes 393224 | tf_op jit(solution)/shard_map/while/body/eval_jaxpr/ppermute | solution.py:14
  102.9 8.5 %collective-permute-start = (f32[2,128,128]{2,1,0:T(8,128)S(1)}, f32[2,128,128]{2,1,0:T(8,128)S(1)}, u32[]{:S(2)}, u32[]{:S(2)}) collective-permute-start(f32[2,128,128]{2,1,0:T(8,128)S(1)} %convolution_add_fusion.20), channel_id=1, source_target_pairs={{2,0},{4,2},{6,4},{8,6},{10,8},{12,10},{14,12},{16,14},{18,16},{20... | collective-permute-start | bytes 393224 | tf_op jit(solution)/shard_map/while/body/eval_jaxpr/ppermute | solution.py:14
  111.6 8.1 %collective-permute-start = (f32[2,128,128]{2,1,0:T(8,128)S(1)}, f32[2,128,128]{2,1,0:T(8,128)S(1)}, u32[]{:S(2)}, u32[]{:S(2)}) collective-permute-start(f32[2,128,128]{2,1,0:T(8,128)S(1)} %convolution_add_fusion.20), channel_id=1, source_target_pairs={{2,0},{4,2},{6,4},{8,6},{10,8},{12,10},{14,12},{16,14},{18,16},{20... | collective-permute-start | bytes 393224 | tf_op jit(solution)/shard_map/while/body/eval_jaxpr/ppermute | solution.py:14
  120.0 8.4 %collective-permute-start = (f32[2,128,128]{2,1,0:T(8,128)S(1)}, f32[2,128,128]{2,1,0:T(8,128)S(1)}, u32[]{:S(2)}, u32[]{:S(2)}) collective-permute-start(f32[2,128,128]{2,1,0:T(8,128)S(1)} %convolution_add_fusion.20), channel_id=1, source_target_pairs={{2,0},{4,2},{6,4},{8,6},{10,8},{12,10},{14,12},{16,14},{18,16},{20... | collective-permute-start | bytes 393224 | tf_op jit(solution)/shard_map/while/body/eval_jaxpr/ppermute | solution.py:14
  128.7 8.7 %collective-permute-start = (f32[2,128,128]{2,1,0:T(8,128)S(1)}, f32[2,128,128]{2,1,0:T(8,128)S(1)}, u32[]{:S(2)}, u32[]{:S(2)}) collective-permute-start(f32[2,128,128]{2,1,0:T(8,128)S(1)} %convolution_add_fusion.20), channel_id=1, source_target_pairs={{2,0},{4,2},{6,4},{8,6},{10,8},{12,10},{14,12},{16,14},{18,16},{20... | collective-permute-start | bytes 393224 | tf_op jit(solution)/shard_map/while/body/eval_jaxpr/ppermute | solution.py:14
  137.6 8.7 %collective-permute-start = (f32[2,128,128]{2,1,0:T(8,128)S(1)}, f32[2,128,128]{2,1,0:T(8,128)S(1)}, u32[]{:S(2)}, u32[]{:S(2)}) collective-permute-start(f32[2,128,128]{2,1,0:T(8,128)S(1)} %convolution_add_fusion.20), channel_id=1, source_target_pairs={{2,0},{4,2},{6,4},{8,6},{10,8},{12,10},{14,12},{16,14},{18,16},{20... | collective-permute-start | bytes 393224 | tf_op jit(solution)/shard_map/while/body/eval_jaxpr/ppermute | solution.py:14
  146.5 8.7 %collective-permute-start = (f32[2,128,128]{2,1,0:T(8,128)S(1)}, f32[2,128,128]{2,1,0:T(8,128)S(1)}, u32[]{:S(2)}, u32[]{:S(2)}) collective-permute-start(f32[2,128,128]{2,1,0:T(8,128)S(1)} %convolution_add_fusion.20), channel_id=1, source_target_pairs={{2,0},{4,2},{6,4},{8,6},{10,8},{12,10},{14,12},{16,14},{18,16},{20... | collective-permute-start | bytes 393224 | tf_op jit(solution)/shard_map/while/body/eval_jaxpr/ppermute | solution.py:14
  155.5 8.8 %collective-permute-start = (f32[2,128,128]{2,1,0:T(8,128)S(1)}, f32[2,128,128]{2,1,0:T(8,128)S(1)}, u32[]{:S(2)}, u32[]{:S(2)}) collective-permute-start(f32[2,128,128]{2,1,0:T(8,128)S(1)} %convolution_add_fusion.20), channel_id=1, source_target_pairs={{2,0},{4,2},{6,4},{8,6},{10,8},{12,10},{14,12},{16,14},{18,16},{20... | collective-permute-start | bytes 393224 | tf_op jit(solution)/shard_map/while/body/eval_jaxpr/ppermute | solution.py:14
  164.3 84.2 %collective-permute-start.21 = (f32[2,2,128]{2,1,0:T(2,128)S(1)}, f32[2,2,128]{2,1,0:T(2,128)S(1)}, u32[]{:S(2)}, u32[]{:S(2)}) collective-permute-start(f32[2,2,128]{2,1,0:T(2,128)S(1)} %get-tuple-element.350), channel_id=1, source_target_pairs={{10,0},{12,2},{14,4},{16,6},{18,8},{20,10},{22,12},{24,14},{26,16}... | collective-permute-start | bytes 6152 | tf_op jit(solution)/shard_map/ppermute | solution.py:14
  249.8 9.6 %collective-permute-start.11 = (bf16[2,128,256]{1,2,0:T(8,128)(2,1)S(1)}, bf16[2,128,256]{1,2,0:T(8,128)(2,1)S(1)}, u32[]{:S(2)}, u32[]{:S(2)}) collective-permute-start(bf16[2,128,256]{1,2,0:T(8,128)(2,1)S(1)} %get-tuple-element.334), channel_id=1, source_target_pairs={{6,0},{8,2},{10,4},{12,6},{14,8},{16,10},{18,12},{20,14},{22,16},{... | collective-permute-start | bytes 393224 | tf_op jit(solution)/shard_map/ppermute | solution.py:14
  251.5 9.1 %collective-permute-start.12 = (bf16[2,128,256]{1,2,0:T(8,128)(2,1)S(1)}, bf16[2,128,256]{1,2,0:T(8,128)(2,1)S(1)}, u32[]{:S(2)}, u32[]{:S(2)}) collective-permute-start(bf16[2,128,256]{1,2,0:T(8,128)(2,1)S(1)} %get-tuple-element.334), channel_id=1, source_target_pairs={{8,0},{10,2},{12,4},{14,6},{16,8},{18,10},{20,12},{22,14},{24,16},... | collective-permute-start | bytes 393224 | tf_op jit(solution)/shard_map/ppermute | solution.py:14
  252.8 18.4 %collective-permute-start.13 = (bf16[2,128,256]{1,2,0:T(8,128)(2,1)S(1)}, bf16[2,128,256]{1,2,0:T(8,128)(2,1)S(1)}, u32[]{:S(2)}, u32[]{:S(2)}) collective-permute-start(bf16[2,128,256]{1,2,0:T(8,128)(2,1)S(1)} %get-tuple-element.334), channel_id=1, source_target_pairs={{10,0},{12,2},{14,4},{16,6},{18,8},{20,10},{22,12},{24,14},{26,16}... | collective-permute-start | bytes 393224 | tf_op jit(solution)/shard_map/ppermute | solution.py:14
  254.8 22.9 %collective-permute-start.14 = (bf16[2,128,256]{1,2,0:T(8,128)(2,1)S(1)}, bf16[2,128,256]{1,2,0:T(8,128)(2,1)S(1)}, u32[]{:S(2)}, u32[]{:S(2)}) collective-permute-start(bf16[2,128,256]{1,2,0:T(8,128)(2,1)S(1)} %get-tuple-element.334), channel_id=1, source_target_pairs={{12,0},{14,2},{16,4},{18,6},{20,8},{22,10},{24,12},{26,14},{28,16}... | collective-permute-start | bytes 393224 | tf_op jit(solution)/shard_map/ppermute | solution.py:14
  256.1 23.6 %collective-permute-start.15 = (bf16[2,128,256]{1,2,0:T(8,128)(2,1)S(1)}, bf16[2,128,256]{1,2,0:T(8,128)(2,1)S(1)}, u32[]{:S(2)}, u32[]{:S(2)}) collective-permute-start(bf16[2,128,256]{1,2,0:T(8,128)(2,1)S(1)} %get-tuple-element.334), channel_id=1, source_target_pairs={{14,0},{16,2},{18,4},{20,6},{22,8},{24,10},{26,12},{28,14},{30,16}... | collective-permute-start | bytes 393224 | tf_op jit(solution)/shard_map/ppermute | solution.py:14
  259.3 22.4 %collective-permute-start.16 = (bf16[2,128,256]{1,2,0:T(8,128)(2,1)S(1)}, bf16[2,128,256]{1,2,0:T(8,128)(2,1)S(1)}, u32[]{:S(2)}, u32[]{:S(2)}) collective-permute-start(bf16[2,128,256]{1,2,0:T(8,128)(2,1)S(1)} %get-tuple-element.334), channel_id=1, source_target_pairs={{16,0},{18,2},{20,4},{22,6},{24,8},{26,10},{28,12},{30,14},{17,1},... | collective-permute-start | bytes 393224 | tf_op jit(solution)/shard_map/ppermute | solution.py:14
  260.7 27.2 %collective-permute-start.1 = (bf16[2,128,256]{1,2,0:T(8,128)(2,1)S(1)}, bf16[2,128,256]{1,2,0:T(8,128)(2,1)}, u32[]{:S(2)}, u32[]{:S(2)}) collective-permute-start(bf16[2,128,256]{1,2,0:T(8,128)(2,1)S(1)} %pad_maximum_fusion), channel_id=1, source_target_pairs={{0,16},{2,18},{4,20},{6,22},{8,24},{10,26},{12,28},{14,30},{1,17},... | collective-permute-start | bytes 393224 | tf_op jit(solution)/shard_map/ppermute | solution.py:14
  271.3 20.5 %collective-permute-start.2 = (bf16[2,128,256]{1,2,0:T(8,128)(2,1)S(1)}, bf16[2,128,256]{1,2,0:T(8,128)(2,1)}, u32[]{:S(2)}, u32[]{:S(2)}) collective-permute-start(bf16[2,128,256]{1,2,0:T(8,128)(2,1)S(1)} %pad_maximum_fusion), channel_id=1, source_target_pairs={{0,14},{2,16},{4,18},{6,20},{8,22},{10,24},{12,26},{14,28},{16,30}... | collective-permute-start | bytes 393224 | tf_op jit(solution)/shard_map/ppermute | solution.py:14
  277.7 16.3 %collective-permute-start.3 = (bf16[2,128,256]{1,2,0:T(8,128)(2,1)S(1)}, bf16[2,128,256]{1,2,0:T(8,128)(2,1)}, u32[]{:S(2)}, u32[]{:S(2)}) collective-permute-start(bf16[2,128,256]{1,2,0:T(8,128)(2,1)S(1)} %pad_maximum_fusion), channel_id=1, source_target_pairs={{0,12},{2,14},{4,16},{6,18},{8,20},{10,22},{12,24},{14,26},{16,28}... | collective-permute-start | bytes 393224 | tf_op jit(solution)/shard_map/ppermute | solution.py:14
  279.7 18.4 %collective-permute-start.4 = (bf16[2,128,256]{1,2,0:T(8,128)(2,1)S(1)}, bf16[2,128,256]{1,2,0:T(8,128)(2,1)}, u32[]{:S(2)}, u32[]{:S(2)}) collective-permute-start(bf16[2,128,256]{1,2,0:T(8,128)(2,1)S(1)} %pad_maximum_fusion), channel_id=1, source_target_pairs={{0,10},{2,12},{4,14},{6,16},{8,18},{10,20},{12,22},{14,24},{16,26}... | collective-permute-start | bytes 393224 | tf_op jit(solution)/shard_map/ppermute | solution.py:14
  281.7 17.3 %collective-permute-start.5 = (bf16[2,128,256]{1,2,0:T(8,128)(2,1)S(1)}, bf16[2,128,256]{1,2,0:T(8,128)(2,1)}, u32[]{:S(2)}, u32[]{:S(2)}) collective-permute-start(bf16[2,128,256]{1,2,0:T(8,128)(2,1)S(1)} %pad_maximum_fusion), channel_id=1, source_target_pairs={{0,8},{2,10},{4,12},{6,14},{8,16},{10,18},{12,20},{14,22},{16,24},... | collective-permute-start | bytes 393224 | tf_op jit(solution)/shard_map/ppermute | solution.py:14
  287.8 12.1 %collective-permute-start.6 = (bf16[2,128,256]{1,2,0:T(8,128)(2,1)S(1)}, bf16[2,128,256]{1,2,0:T(8,128)(2,1)S(1)}, u32[]{:S(2)}, u32[]{:S(2)}) collective-permute-start(bf16[2,128,256]{1,2,0:T(8,128)(2,1)S(1)} %pad_maximum_fusion), channel_id=1, source_target_pairs={{0,6},{2,8},{4,10},{6,12},{8,14},{10,16},{12,18},{14,20},{16,22},{... | collective-permute-start | bytes 393224 | tf_op jit(solution)/shard_map/ppermute | solution.py:14
  291.8 8.3 %collective-permute-start.7 = (bf16[2,128,256]{1,2,0:T(8,128)(2,1)S(1)}, bf16[2,128,256]{1,2,0:T(8,128)(2,1)S(1)}, u32[]{:S(2)}, u32[]{:S(2)}) collective-permute-start(bf16[2,128,256]{1,2,0:T(8,128)(2,1)S(1)} %pad_maximum_fusion), channel_id=1, source_target_pairs={{0,4},{2,6},{4,8},{6,10},{8,12},{10,14},{12,16},{14,18},{16,20},{1... | collective-permute-start | bytes 393224 | tf_op jit(solution)/shard_map/ppermute | solution.py:14
  (41 other events, 303.9 us)
Sparse Core Ops, SparseCore 0:
  288.0 4.5 reduce-scatter.1
where the time goes:
time: 313 us; the launch traced here: 311 us
  waiting for transfers between devices  112 us (36%)
  starting transfers between devices  70.6 us (23%)
  blocking collectives  54.2 us (17%)
  matrix products  31.3 us (10%)
  local copies, waits for them, and re-layouts  19.6 us (6%)
  between operations  15.6 us (5%)
  other arithmetic  7.44 us (2%)
    ppermute x39, waiting for transfers between devices, from_behind(): return lax.ppermute(block, axis, route)  112 us
    ppermute x39, starting transfers between devices, from_behind(): return lax.ppermute(block, axis, route)  70.6 us
    all_gather x1, blocking collectives, per_device(): row_piece = lax.all_gather(w_kv, 'seq', axis=0, tiled=True)  54.2 us
    dot_general x53, matrix products, matmul(): return jnp.dot(left_side, right_side, precision=HIGH)  21.9 us
    unnamed x98, local copies, waits for them, and re-layouts  11.8 us
  transfers between devices with their start and end apart: 40, of which 17 were waited for; matrix products, arithmetic and copies ran while one was open for 16% of the time, Pallas kernels for 0%

commit v1 on v0

--- a/solution.py
+++ b/solution.py
@@ -1,3 +1,4 @@
+import functools
 import jax
 import jax.numpy as jnp
 from jax import lax
@@ -6,6 +7,26 @@
 BLOCK = 64
 WINDOW = 1024
 HIGH = lax.Precision.HIGHEST
+
+
+def obtain_gates(panel, device_axis):
+    block_now = lax.axis_size(device_axis)
+    m_next = lax.axis_index(device_axis)
+    vec_out, tmp = (block_now, m_next)
+    long_array, local_now = (panel, 1)
+    while local_now < vec_out:
+        stack_in = []
+        for dev in range(vec_out):
+            stack_in.append((dev, dev ^ local_now))
+        ready = lax.ppermute(long_array, device_axis, stack_in)
+        aux = jnp.concatenate([long_array, ready], axis=0)
+        after = jnp.concatenate([ready, long_array], axis=0)
+        long_array = jnp.where(tmp & local_now == 0, aux, after)
+        local_now = 2 * local_now
+    return long_array
+
+
+wait_the_ways = functools.partial(obtain_gates, device_axis="seq")
 
 
 def from_behind(block, axis, distance):
@@ -182,7 +203,7 @@
     key_grad = own_k.reshape(row_count, column_count).astype(jnp.bfloat16)
     value_grad = own_v.reshape(row_count, column_count).astype(jnp.bfloat16)
     attn_dq = grad_q.reshape(row_count, column_count).astype(jnp.bfloat16)
-    row_piece = lax.all_gather(w_kv, "seq", axis=0, tiled=True)
+    row_piece = wait_the_ways(w_kv)
     from_keys = lax.dot_general(
         row_piece[:, 0, :], key_grad, (((1,), (1,)), ((), ())), preferred_element_type=jnp.float32
     )

time: 313 us -> 302 us (0.965)
  blocking collectives: 54.2 us -> 0 us
  waiting for transfers between devices: 112 us -> 141 us
  starting transfers between devices: 70.6 us -> 82.4 us
  local copies, waits for them, and re-layouts: 19.6 us -> 16.3 us
  other arithmetic: 7.44 us -> 10.7 us
    all_gather x1 -> x0, blocking collectives: 54.2 us -> none  [per_device(): row_piece = lax.all_gather(w_kv, 'seq', axis=0, tiled=True)]
    ppermute x0 -> x4, waiting for transfers between devices: none -> 15.5 us  [obtain_gates(): ready = lax.ppermute(long_array, device_axis, stack_in)]
    ppermute x39, waiting for transfers between devices: 112 us -> 121 us  [from_behind(): return lax.ppermute(block, axis, route)]
    ppermute x0 -> x4, starting transfers between devices: none -> 8.16 us  [obtain_gates(): ready = lax.ppermute(long_array, device_axis, stack_in)]
    reduce_scatter x1, waiting for transfers between devices: 0.01 us -> 5.27 us  [per_device(): lax.psum_scatter(partial_value, 'head', scatter_dimension=0, tiled=True)]
    ppermute x39, starting transfers between devices: 70.6 us -> 74.2 us  [from_behind(): return lax.ppermute(block, axis, route)]
    unnamed x98 -> x113, local copies, waits for them, and re-layouts: 11.8 us -> 9.1 us
  transfers between devices with their start and end apart: 40 -> 44, of which waited for: 17 -> 22; matrix products, arithmetic and copies ran while one was open for 16% -> 17% of each run, Pallas kernels for 0% -> 0%
where the time goes in v1:
time: 302 us; the launch traced here: 300 us
  waiting for transfers between devices  141 us (47%)
  starting transfers between devices  82.4 us (27%)
  matrix products  33.3 us (11%)
  local copies, waits for them, and re-layouts  16.3 us (5%)
  between operations  15.7 us (5%)
  other arithmetic  10.7 us (4%)
    ppermute x39, waiting for transfers between devices, from_behind(): return lax.ppermute(block, axis, route)  121 us
    ppermute x39, starting transfers between devices, from_behind(): return lax.ppermute(block, axis, route)  74.2 us
    dot_general x53, matrix products, matmul(): return jnp.dot(left_side, right_side, precision=HIGH)  22.4 us
    ppermute x4, waiting for transfers between devices, obtain_gates(): ready = lax.ppermute(long_array, device_axis, stack_in)  15.5 us
    unnamed x113, local copies, waits for them, and re-layouts  9.1 us
    ppermute x4, starting transfers between devices, obtain_gates(): ready = lax.ppermute(long_array, device_axis, stack_in)  8.16 us
  transfers between devices with their start and end apart: 44, of which 22 were waited for; matrix products, arithmetic and copies ran while one was open for 17% of the time, Pallas kernels for 0%

profile of v1, /device:TPU:0, one launch (start us, length us, event | category | flops | bytes accessed | tf_op | source)
XLA Modules:
  0.0 300.3 jit_solution(8211843702752108470)
XLA Ops:
  26.0 1.9 fusion.49
  32.0 133.4 %while.43 = (s32[]{:T(128)}, f32[2,128,128]{2,1,0:T(8,128)S(1)}, f32[2,128,128]{2,1,0:T(8,128)S(1)}, f32[2,128,128]{2,1,0:T(8,128)S(1)}, s32[]{:T(128)}) while((s32[]{:T(128)}, f32[2,128,128]{2,1,0:T(8,128)S(1)}, f32[2,128,128]{2,1,0:T(8,128)S(1)}, f32[2,128,128]{2,1,0:T(8,128)S(1)}, s32[]{:T(128)}) %tuple.116), condition=%wide.region_9.10_spmd, body=%wide.region_8.9_spmd.sunk | while | flops 50364416 | bytes 1048677 | solution.py:254
  33.6 7.7 %collective-permute-done = f32[2,128,128]{2,1,0:T(8,128)S(1)} collective-permute-done((f32[2,128,128]{2,1,0:T(8,128)S(1)}, f32[2,128,128]{2,1,0:T(8,128)S(1)}, u32[]{:S(2)}, u32[]{:S(2)}) %collective-permute-start) | collective-permute-done | bytes 131104 | tf_op jit(solution)/shard_map/while/body/eval_jaxpr/ppermute | solution.py:35
  42.9 6.8 %collective-permute-done = f32[2,128,128]{2,1,0:T(8,128)S(1)} collective-permute-done((f32[2,128,128]{2,1,0:T(8,128)S(1)}, f32[2,128,128]{2,1,0:T(8,128)S(1)}, u32[]{:S(2)}, u32[]{:S(2)}) %collective-permute-start) | collective-permute-done | bytes 131104 | tf_op jit(solution)/shard_map/while/body/eval_jaxpr/ppermute | solution.py:35
  51.3 6.5 %collective-permute-done = f32[2,128,128]{2,1,0:T(8,128)S(1)} collective-permute-done((f32[2,128,128]{2,1,0:T(8,128)S(1)}, f32[2,128,128]{2,1,0:T(8,128)S(1)}, u32[]{:S(2)}, u32[]{:S(2)}) %collective-permute-start) | collective-permute-done | bytes 131104 | tf_op jit(solution)/shard_map/while/body/eval_jaxpr/ppermute | solution.py:35
  59.3 6.5 %collective-permute-done = f32[2,128,128]{2,1,0:T(8,128)S(1)} collective-permute-done((f32[2,128,128]{2,1,0:T(8,128)S(1)}, f32[2,128,128]{2,1,0:T(8,128)S(1)}, u32[]{:S(2)}, u32[]{:S(2)}) %collective-permute-start) | collective-permute-done | bytes 131104 | tf_op jit(solution)/shard_map/while/body/eval_jaxpr/ppermute | solution.py:35
  67.4 6.9 %collective-permute-done = f32[2,128,128]{2,1,0:T(8,128)S(1)} collective-permute-done((f32[2,128,128]{2,1,0:T(8,128)S(1)}, f32[2,128,128]{2,1,0:T(8,128)S(1)}, u32[]{:S(2)}, u32[]{:S(2)}) %collective-permute-start) | collective-permute-done | bytes 131104 | tf_op jit(solution)/shard_map/while/body/eval_jaxpr/ppermute | solution.py:35
  75.8 7.4 %collective-permute-done = f32[2,128,128]{2,1,0:T(8,128)S(1)} collective-permute-done((f32[2,128,128]{2,1,0:T(8,128)S(1)}, f32[2,128,128]{2,1,0:T(8,128)S(1)}, u32[]{:S(2)}, u32[]{:S(2)}) %collective-permute-start) | collective-permute-done | bytes 131104 | tf_op jit(solution)/shard_map/while/body/eval_jaxpr/ppermute | solution.py:35
  84.8 8.7 %collective-permute-done = f32[2,128,128]{2,1,0:T(8,128)S(1)} collective-permute-done((f32[2,128,128]{2,1,0:T(8,128)S(1)}, f32[2,128,128]{2,1,0:T(8,128)S(1)}, u32[]{:S(2)}, u32[]{:S(2)}) %collective-permute-start) | collective-permute-done | bytes 131104 | tf_op jit(solution)/shard_map/while/body/eval_jaxpr/ppermute | solution.py:35
  95.0 8.8 %collective-permute-done = f32[2,128,128]{2,1,0:T(8,128)S(1)} collective-permute-done((f32[2,128,128]{2,1,0:T(8,128)S(1)}, f32[2,128,128]{2,1,0:T(8,128)S(1)}, u32[]{:S(2)}, u32[]{:S(2)}) %collective-permute-start) | collective-permute-done | bytes 131104 | tf_op jit(solution)/shard_map/while/body/eval_jaxpr/ppermute | solution.py:35
  105.3 7.2 %collective-permute-done = f32[2,128,128]{2,1,0:T(8,128)S(1)} collective-permute-done((f32[2,128,128]{2,1,0:T(8,128)S(1)}, f32[2,128,128]{2,1,0:T(8,128)S(1)}, u32[]{:S(2)}, u32[]{:S(2)}) %collective-permute-start) | collective-permute-done | bytes 131104 | tf_op jit(solution)/shard_map/while/body/eval_jaxpr/ppermute | solution.py:35
  114.1 6.8 %collective-permute-done = f32[2,128,128]{2,1,0:T(8,128)S(1)} collective-permute-done((f32[2,128,128]{2,1,0:T(8,128)S(1)}, f32[2,128,128]{2,1,0:T(8,128)S(1)}, u32[]{:S(2)}, u32[]{:S(2)}) %collective-permute-start) | collective-permute-done | bytes 131104 | tf_op jit(solution)/shard_map/while/body/eval_jaxpr/ppermute | solution.py:35
  122.5 7.1 %collective-permute-done = f32[2,128,128]{2,1,0:T(8,128)S(1)} collective-permute-done((f32[2,128,128]{2,1,0:T(8,128)S(1)}, f32[2,128,128]{2,1,0:T(8,128)S(1)}, u32[]{:S(2)}, u32[]{:S(2)}) %collective-permute-start) | collective-permute-done | bytes 131104 | tf_op jit(solution)/shard_map/while/body/eval_jaxpr/ppermute | solution.py:35
  131.1 7.4 %collective-permute-done = f32[2,128,128]{2,1,0:T(8,128)S(1)} collective-permute-done((f32[2,128,128]{2,1,0:T(8,128)S(1)}, f32[2,128,128]{2,1,0:T(8,128)S(1)}, u32[]{:S(2)}, u32[]{:S(2)}) %collective-permute-start) | collective-permute-done | bytes 131104 | tf_op jit(solution)/shard_map/while/body/eval_jaxpr/ppermute | solution.py:35
  140.0 7.4 %collective-permute-done = f32[2,128,128]{2,1,0:T(8,128)S(1)} collective-permute-done((f32[2,128,128]{2,1,0:T(8,128)S(1)}, f32[2,128,128]{2,1,0:T(8,128)S(1)}, u32[]{:S(2)}, u32[]{:S(2)}) %collective-permute-start) | collective-permute-done | bytes 131104 | tf_op jit(solution)/shard_map/while/body/eval_jaxpr/ppermute | solution.py:35
  149.0 7.4 %collective-permute-done = f32[2,128,128]{2,1,0:T(8,128)S(1)} collective-permute-done((f32[2,128,128]{2,1,0:T(8,128)S(1)}, f32[2,128,128]{2,1,0:T(8,128)S(1)}, u32[]{:S(2)}, u32[]{:S(2)}) %collective-permute-start) | collective-permute-done | bytes 131104 | tf_op jit(solution)/shard_map/while/body/eval_jaxpr/ppermute | solution.py:35
  157.9 7.5 %collective-permute-done = f32[2,128,128]{2,1,0:T(8,128)S(1)} collective-permute-done((f32[2,128,128]{2,1,0:T(8,128)S(1)}, f32[2,128,128]{2,1,0:T(8,128)S(1)}, u32[]{:S(2)}, u32[]{:S(2)}) %collective-permute-start) | collective-permute-done | bytes 131104 | tf_op jit(solution)/shard_map/while/body/eval_jaxpr/ppermute | solution.py:35
  199.9 5.5 %collective-permute-done.26 = f32[2,2,128]{2,1,0:T(2,128)S(1)} collective-permute-done((f32[2,2,128]{2,1,0:T(2,128)}, f32[2,2,128]{2,1,0:T(2,128)S(1)}, u32[]{:S(2)}, u32[]{:S(2)}) %collective-permute-start.26) | collective-permute-done | bytes 2080 | tf_op jit(solution)/shard_map/ppermute | solution.py:35
  206.7 4.5 %collective-permute-done.27 = f32[2,2,128]{2,1,0:T(2,128)S(1)} collective-permute-done((f32[2,2,128]{2,1,0:T(2,128)}, f32[2,2,128]{2,1,0:T(2,128)S(1)}, u32[]{:S(2)}, u32[]{:S(2)}) %collective-permute-start.27) | collective-permute-done | bytes 2080 | tf_op jit(solution)/shard_map/ppermute | solution.py:35
  212.7 4.9 %collective-permute-done.9 = bf16[32,2,256]{2,0,1:T(8,128)(2,1)S(1)} collective-permute-done((bf16[32,2,256]{2,0,1:T(8,128)(2,1)S(1)}, bf16[32,2,256]{2,0,1:T(8,128)(2,1)S(1)}, u32[]{:S(2)}, u32[]{:S(2)}) %collective-permute-start.9) | collective-permute-done | bytes 32800 | tf_op jit(solution)/shard_map/ppermute | solution.py:21
  218.1 3.8 %collective-permute-done.10 = bf16[64,2,256]{2,0,1:T(8,128)(2,1)S(1)} collective-permute-done((bf16[64,2,256]{2,0,1:T(8,128)(2,1)S(1)}, bf16[64,2,256]{2,0,1:T(8,128)(2,1)S(1)}, u32[]{:S(2)}, u32[]{:S(2)}) %collective-permute-start.10) | collective-permute-done | bytes 65568 | tf_op jit(solution)/shard_map/ppermute | solution.py:21
  227.9 14.8 %collective-permute-start.1 = (bf16[2,128,256]{1,2,0:T(8,128)(2,1)}, bf16[2,128,256]{1,2,0:T(8,128)(2,1)S(1)}, u32[]{:S(2)}, u32[]{:S(2)}) collective-permute-start(bf16[2,128,256]{1,2,0:T(8,128)(2,1)} %pad_maximum_fusion), channel_id=1, source_target_pairs={{0,16},{2,18},{4,20},{6,22},{8,24},{10,26},{12,28},{14,30},{1,17},... | collective-permute-start | bytes 393224 | tf_op jit(solution)/shard_map/ppermute | solution.py:35
  242.8 5.7 %collective-permute-start.2 = (bf16[2,128,256]{1,2,0:T(8,128)(2,1)}, bf16[2,128,256]{1,2,0:T(8,128)(2,1)S(1)}, u32[]{:S(2)}, u32[]{:S(2)}) collective-permute-start(bf16[2,128,256]{1,2,0:T(8,128)(2,1)} %pad_maximum_fusion), channel_id=1, source_target_pairs={{0,14},{2,16},{4,18},{6,20},{8,22},{10,24},{12,26},{14,28},{16,30}... | collective-permute-start | bytes 393224 | tf_op jit(solution)/shard_map/ppermute | solution.py:35
  251.3 2.5 collective-permute-start.5
  254.0 3.9 %collective-permute-start.6 = (bf16[2,128,256]{1,2,0:T(8,128)(2,1)}, bf16[2,128,256]{1,2,0:T(8,128)(2,1)S(1)}, u32[]{:S(2)}, u32[]{:S(2)}) collective-permute-start(bf16[2,128,256]{1,2,0:T(8,128)(2,1)} %pad_maximum_fusion), channel_id=1, source_target_pairs={{0,6},{2,8},{4,10},{6,12},{8,14},{10,16},{12,18},{14,20},{16,22},{... | collective-permute-start | bytes 393224 | tf_op jit(solution)/shard_map/ppermute | solution.py:35
  257.9 1.6 collective-permute-start.7
  259.5 2.8 collective-permute-start.8
  262.4 1.8 collective-permute-start.11
  266.7 2.2 fusion.33
  270.1 5.8 %collective-permute-start.12 = (bf16[256,2,256]{2,0,1:T(8,128)(2,1)S(1)}, bf16[256,2,256]{2,0,1:T(8,128)(2,1)S(1)}, u32[]{:S(2)}, u32[]{:S(2)}) collective-permute-start(bf16[256,2,256]{2,0,1:T(8,128)(2,1)S(1)} %maximum_select_fusion.1), channel_id=1, source_target_pairs={{0,16},{2,18},{4,20},{6,22},{8,24},{10,26},{12,28},{14,30},{16,0},... | collective-permute-start | bytes 786440 | tf_op jit(solution)/shard_map/ppermute | solution.py:21
  276.3 6.8 %collective-permute-done.12 = bf16[256,2,256]{2,0,1:T(8,128)(2,1)S(1)} collective-permute-done((bf16[256,2,256]{2,0,1:T(8,128)(2,1)S(1)}, bf16[256,2,256]{2,0,1:T(8,128)(2,1)S(1)}, u32[]{:S(2)}, u32[]{:S(2)}) %collective-permute-start.12) | collective-permute-done | bytes 262176 | tf_op jit(solution)/shard_map/ppermute | solution.py:21
  286.7 5.3 %reduce-scatter.2.cloned.1.call-done = f32[256,128]{1,0:T(8,128)} async-done(((f32[512,128]{1,0:T(8,128)}), f32[256,128]{1,0:T(8,128)}) %reduce-scatter.2.cloned.1.call-update) | async-done | bytes 131088 | tf_op jit(solution)/shard_map/reduce_scatter | solution.py:213
  (333 shorter events, 102.6 us)
Async XLA Ops:
  7.2 284.8 %reduce-scatter.2.cloned.1.call-start = ((), (), s32[]{:S(2)}) async-start(), calls=%async_computation.1 | async-start | bytes 393216 | tf_op jit(solution)/shard_map/reduce_scatter | solution.py:213
  10.6 179.3 %collective-permute-start.21 = (f32[2,2,128]{2,1,0:T(2,128)}, f32[2,2,128]{2,1,0:T(2,128)}, u32[]{:S(2)}, u32[]{:S(2)}) collective-permute-start(f32[2,2,128]{2,1,0:T(2,128)} %get-tuple-element.350), channel_id=1, source_target_pairs={{2,0},{4,2},{6,4},{8,6},{10,8},{12,10},{14,12},{16,14},{18,16},{20... | collective-permute-start | bytes 6152 | tf_op jit(solution)/shard_map/ppermute | solution.py:35
  11.9 180.0 %collective-permute-start.22 = (f32[2,2,128]{2,1,0:T(2,128)}, f32[2,2,128]{2,1,0:T(2,128)}, u32[]{:S(2)}, u32[]{:S(2)}) collective-permute-start(f32[2,2,128]{2,1,0:T(2,128)} %get-tuple-element.350), channel_id=1, source_target_pairs={{4,0},{6,2},{8,4},{10,6},{12,8},{14,10},{16,12},{18,14},{20,16},{2... | collective-permute-start | bytes 6152 | tf_op jit(solution)/shard_map/ppermute | solution.py:35
  13.2 180.7 %collective-permute-start.23 = (f32[2,2,128]{2,1,0:T(2,128)}, f32[2,2,128]{2,1,0:T(2,128)}, u32[]{:S(2)}, u32[]{:S(2)}) collective-permute-start(f32[2,2,128]{2,1,0:T(2,128)} %get-tuple-element.350), channel_id=1, source_target_pairs={{6,0},{8,2},{10,4},{12,6},{14,8},{16,10},{18,12},{20,14},{22,16},{... | collective-permute-start | bytes 6152 | tf_op jit(solution)/shard_map/ppermute | solution.py:35
  14.5 181.5 %collective-permute-start.24 = (f32[2,2,128]{2,1,0:T(2,128)}, f32[2,2,128]{2,1,0:T(2,128)}, u32[]{:S(2)}, u32[]{:S(2)}) collective-permute-start(f32[2,2,128]{2,1,0:T(2,128)} %get-tuple-element.350), channel_id=1, source_target_pairs={{8,0},{10,2},{12,4},{14,6},{16,8},{18,10},{20,12},{22,14},{24,16},... | collective-permute-start | bytes 6152 | tf_op jit(solution)/shard_map/ppermute | solution.py:35
  32.3 9.0 %collective-permute-start = (f32[2,128,128]{2,1,0:T(8,128)S(1)}, f32[2,128,128]{2,1,0:T(8,128)S(1)}, u32[]{:S(2)}, u32[]{:S(2)}) collective-permute-start(f32[2,128,128]{2,1,0:T(8,128)S(1)} %convolution_add_fusion.20), channel_id=1, source_target_pairs={{2,0},{4,2},{6,4},{8,6},{10,8},{12,10},{14,12},{16,14},{18,16},{20... | collective-permute-start | bytes 393224 | tf_op jit(solution)/shard_map/while/body/eval_jaxpr/ppermute | solution.py:35
  74.5 8.7 %collective-permute-start = (f32[2,128,128]{2,1,0:T(8,128)S(1)}, f32[2,128,128]{2,1,0:T(8,128)S(1)}, u32[]{:S(2)}, u32[]{:S(2)}) collective-permute-start(f32[2,128,128]{2,1,0:T(8,128)S(1)} %convolution_add_fusion.20), channel_id=1, source_target_pairs={{2,0},{4,2},{6,4},{8,6},{10,8},{12,10},{14,12},{16,14},{18,16},{20... | collective-permute-start | bytes 393224 | tf_op jit(solution)/shard_map/while/body/eval_jaxpr/ppermute | solution.py:35
  83.5 10.0 %collective-permute-start = (f32[2,128,128]{2,1,0:T(8,128)S(1)}, f32[2,128,128]{2,1,0:T(8,128)S(1)}, u32[]{:S(2)}, u32[]{:S(2)}) collective-permute-start(f32[2,128,128]{2,1,0:T(8,128)S(1)} %convolution_add_fusion.20), channel_id=1, source_target_pairs={{2,0},{4,2},{6,4},{8,6},{10,8},{12,10},{14,12},{16,14},{18,16},{20... | collective-permute-start | bytes 393224 | tf_op jit(solution)/shard_map/while/body/eval_jaxpr/ppermute | solution.py:35
  93.7 10.1 %collective-permute-start = (f32[2,128,128]{2,1,0:T(8,128)S(1)}, f32[2,128,128]{2,1,0:T(8,128)S(1)}, u32[]{:S(2)}, u32[]{:S(2)}) collective-permute-start(f32[2,128,128]{2,1,0:T(8,128)S(1)} %convolution_add_fusion.20), channel_id=1, source_target_pairs={{2,0},{4,2},{6,4},{8,6},{10,8},{12,10},{14,12},{16,14},{18,16},{20... | collective-permute-start | bytes 393224 | tf_op jit(solution)/shard_map/while/body/eval_jaxpr/ppermute | solution.py:35
  129.8 8.7 %collective-permute-start = (f32[2,128,128]{2,1,0:T(8,128)S(1)}, f32[2,128,128]{2,1,0:T(8,128)S(1)}, u32[]{:S(2)}, u32[]{:S(2)}) collective-permute-start(f32[2,128,128]{2,1,0:T(8,128)S(1)} %convolution_add_fusion.20), channel_id=1, source_target_pairs={{2,0},{4,2},{6,4},{8,6},{10,8},{12,10},{14,12},{16,14},{18,16},{20... | collective-permute-start | bytes 393224 | tf_op jit(solution)/shard_map/while/body/eval_jaxpr/ppermute | solution.py:35
  138.7 8.7 %collective-permute-start = (f32[2,128,128]{2,1,0:T(8,128)S(1)}, f32[2,128,128]{2,1,0:T(8,128)S(1)}, u32[]{:S(2)}, u32[]{:S(2)}) collective-permute-start(f32[2,128,128]{2,1,0:T(8,128)S(1)} %convolution_add_fusion.20), channel_id=1, source_target_pairs={{2,0},{4,2},{6,4},{8,6},{10,8},{12,10},{14,12},{16,14},{18,16},{20... | collective-permute-start | bytes 393224 | tf_op jit(solution)/shard_map/while/body/eval_jaxpr/ppermute | solution.py:35
  147.7 8.7 %collective-permute-start = (f32[2,128,128]{2,1,0:T(8,128)S(1)}, f32[2,128,128]{2,1,0:T(8,128)S(1)}, u32[]{:S(2)}, u32[]{:S(2)}) collective-permute-start(f32[2,128,128]{2,1,0:T(8,128)S(1)} %convolution_add_fusion.20), channel_id=1, source_target_pairs={{2,0},{4,2},{6,4},{8,6},{10,8},{12,10},{14,12},{16,14},{18,16},{20... | collective-permute-start | bytes 393224 | tf_op jit(solution)/shard_map/while/body/eval_jaxpr/ppermute | solution.py:35
  156.6 8.8 %collective-permute-start = (f32[2,128,128]{2,1,0:T(8,128)S(1)}, f32[2,128,128]{2,1,0:T(8,128)S(1)}, u32[]{:S(2)}, u32[]{:S(2)}) collective-permute-start(f32[2,128,128]{2,1,0:T(8,128)S(1)} %convolution_add_fusion.20), channel_id=1, source_target_pairs={{2,0},{4,2},{6,4},{8,6},{10,8},{12,10},{14,12},{16,14},{18,16},{20... | collective-permute-start | bytes 393224 | tf_op jit(solution)/shard_map/while/body/eval_jaxpr/ppermute | solution.py:35
  165.4 32.5 %collective-permute-start.25 = (f32[2,2,128]{2,1,0:T(2,128)}, f32[2,2,128]{2,1,0:T(2,128)}, u32[]{:S(2)}, u32[]{:S(2)}) collective-permute-start(f32[2,2,128]{2,1,0:T(2,128)} %get-tuple-element.350), channel_id=1, source_target_pairs={{10,0},{12,2},{14,4},{16,6},{18,8},{20,10},{22,12},{24,14},{26,16}... | collective-permute-start | bytes 6152 | tf_op jit(solution)/shard_map/ppermute | solution.py:35
  189.8 15.6 %collective-permute-start.26 = (f32[2,2,128]{2,1,0:T(2,128)}, f32[2,2,128]{2,1,0:T(2,128)S(1)}, u32[]{:S(2)}, u32[]{:S(2)}) collective-permute-start(f32[2,2,128]{2,1,0:T(2,128)} %get-tuple-element.350), channel_id=1, source_target_pairs={{12,0},{14,2},{16,4},{18,6},{20,8},{22,10},{24,12},{26,14},{28,16}... | collective-permute-start | bytes 6152 | tf_op jit(solution)/shard_map/ppermute | solution.py:35
  191.8 19.4 %collective-permute-start.27 = (f32[2,2,128]{2,1,0:T(2,128)}, f32[2,2,128]{2,1,0:T(2,128)S(1)}, u32[]{:S(2)}, u32[]{:S(2)}) collective-permute-start(f32[2,2,128]{2,1,0:T(2,128)} %get-tuple-element.350), channel_id=1, source_target_pairs={{14,0},{16,2},{18,4},{20,6},{22,8},{24,10},{26,12},{28,14},{30,16}... | collective-permute-start | bytes 6152 | tf_op jit(solution)/shard_map/ppermute | solution.py:35
  193.8 18.8 %collective-permute-start.28 = (f32[2,2,128]{2,1,0:T(2,128)}, f32[2,2,128]{2,1,0:T(2,128)S(1)}, u32[]{:S(2)}, u32[]{:S(2)}) collective-permute-start(f32[2,2,128]{2,1,0:T(2,128)} %get-tuple-element.350), channel_id=1, source_target_pairs={{16,0},{18,2},{20,4},{22,6},{24,8},{26,10},{28,12},{30,14},{17,1},... | collective-permute-start | bytes 6152 | tf_op jit(solution)/shard_map/ppermute | solution.py:35
  196.0 27.9 %collective-permute-start.13 = (bf16[2,128,256]{1,2,0:T(8,128)(2,1)S(1)}, bf16[2,128,256]{1,2,0:T(8,128)(2,1)S(1)}, u32[]{:S(2)}, u32[]{:S(2)}) collective-permute-start(bf16[2,128,256]{1,2,0:T(8,128)(2,1)S(1)} %get-tuple-element.334), channel_id=1, source_target_pairs={{2,0},{4,2},{6,4},{8,6},{10,8},{12,10},{14,12},{16,14},{18,16},{20... | collective-permute-start | bytes 393224 | tf_op jit(solution)/shard_map/ppermute | solution.py:35
  198.0 27.2 %collective-permute-start.14 = (bf16[2,128,256]{1,2,0:T(8,128)(2,1)S(1)}, bf16[2,128,256]{1,2,0:T(8,128)(2,1)S(1)}, u32[]{:S(2)}, u32[]{:S(2)}) collective-permute-start(bf16[2,128,256]{1,2,0:T(8,128)(2,1)S(1)} %get-tuple-element.334), channel_id=1, source_target_pairs={{4,0},{6,2},{8,4},{10,6},{12,8},{14,10},{16,12},{18,14},{20,16},{2... | collective-permute-start | bytes 393224 | tf_op jit(solution)/shard_map/ppermute | solution.py:35
  205.4 21.1 %collective-permute-start.15 = (bf16[2,128,256]{1,2,0:T(8,128)(2,1)S(1)}, bf16[2,128,256]{1,2,0:T(8,128)(2,1)S(1)}, u32[]{:S(2)}, u32[]{:S(2)}) collective-permute-start(bf16[2,128,256]{1,2,0:T(8,128)(2,1)S(1)} %get-tuple-element.334), channel_id=1, source_target_pairs={{6,0},{8,2},{10,4},{12,6},{14,8},{16,10},{18,12},{20,14},{22,16},{... | collective-permute-start | bytes 393224 | tf_op jit(solution)/shard_map/ppermute | solution.py:35
  211.3 16.6 %collective-permute-start.16 = (bf16[2,128,256]{1,2,0:T(8,128)(2,1)S(1)}, bf16[2,128,256]{1,2,0:T(8,128)(2,1)S(1)}, u32[]{:S(2)}, u32[]{:S(2)}) collective-permute-start(bf16[2,128,256]{1,2,0:T(8,128)(2,1)S(1)} %get-tuple-element.334), channel_id=1, source_target_pairs={{8,0},{10,2},{12,4},{14,6},{16,8},{18,10},{20,12},{22,14},{24,16},... | collective-permute-start | bytes 393224 | tf_op jit(solution)/shard_map/ppermute | solution.py:35
  221.9 20.9 %collective-permute-start.17 = (bf16[2,128,256]{1,2,0:T(8,128)(2,1)S(1)}, bf16[2,128,256]{1,2,0:T(8,128)(2,1)S(1)}, u32[]{:S(2)}, u32[]{:S(2)}) collective-permute-start(bf16[2,128,256]{1,2,0:T(8,128)(2,1)S(1)} %get-tuple-element.334), channel_id=1, source_target_pairs={{10,0},{12,2},{14,4},{16,6},{18,8},{20,10},{22,12},{24,14},{26,16}... | collective-permute-start | bytes 393224 | tf_op jit(solution)/shard_map/ppermute | solution.py:35
  223.9 24.7 %collective-permute-start.18 = (bf16[2,128,256]{1,2,0:T(8,128)(2,1)S(1)}, bf16[2,128,256]{1,2,0:T(8,128)(2,1)S(1)}, u32[]{:S(2)}, u32[]{:S(2)}) collective-permute-start(bf16[2,128,256]{1,2,0:T(8,128)(2,1)S(1)} %get-tuple-element.334), channel_id=1, source_target_pairs={{12,0},{14,2},{16,4},{18,6},{20,8},{22,10},{24,12},{26,14},{28,16}... | collective-permute-start | bytes 393224 | tf_op jit(solution)/shard_map/ppermute | solution.py:35
  225.2 24.7 %collective-permute-start.19 = (bf16[2,128,256]{1,2,0:T(8,128)(2,1)S(1)}, bf16[2,128,256]{1,2,0:T(8,128)(2,1)S(1)}, u32[]{:S(2)}, u32[]{:S(2)}) collective-permute-start(bf16[2,128,256]{1,2,0:T(8,128)(2,1)S(1)} %get-tuple-element.334), channel_id=1, source_target_pairs={{14,0},{16,2},{18,4},{20,6},{22,8},{24,10},{26,12},{28,14},{30,16}... | collective-permute-start | bytes 393224 | tf_op jit(solution)/shard_map/ppermute | solution.py:35
  226.6 24.7 %collective-permute-start.20 = (bf16[2,128,256]{1,2,0:T(8,128)(2,1)S(1)}, bf16[2,128,256]{1,2,0:T(8,128)(2,1)S(1)}, u32[]{:S(2)}, u32[]{:S(2)}) collective-permute-start(bf16[2,128,256]{1,2,0:T(8,128)(2,1)S(1)} %get-tuple-element.334), channel_id=1, source_target_pairs={{16,0},{18,2},{20,4},{22,6},{24,8},{26,10},{28,12},{30,14},{17,1},... | collective-permute-start | bytes 393224 | tf_op jit(solution)/shard_map/ppermute | solution.py:35
  227.9 26.0 %collective-permute-start.1 = (bf16[2,128,256]{1,2,0:T(8,128)(2,1)}, bf16[2,128,256]{1,2,0:T(8,128)(2,1)S(1)}, u32[]{:S(2)}, u32[]{:S(2)}) collective-permute-start(bf16[2,128,256]{1,2,0:T(8,128)(2,1)} %pad_maximum_fusion), channel_id=1, source_target_pairs={{0,16},{2,18},{4,20},{6,22},{8,24},{10,26},{12,28},{14,30},{1,17},... | collective-permute-start | bytes 393224 | tf_op jit(solution)/shard_map/ppermute | solution.py:35
  242.8 15.0 %collective-permute-start.2 = (bf16[2,128,256]{1,2,0:T(8,128)(2,1)}, bf16[2,128,256]{1,2,0:T(8,128)(2,1)S(1)}, u32[]{:S(2)}, u32[]{:S(2)}) collective-permute-start(bf16[2,128,256]{1,2,0:T(8,128)(2,1)} %pad_maximum_fusion), channel_id=1, source_target_pairs={{0,14},{2,16},{4,18},{6,20},{8,22},{10,24},{12,26},{14,28},{16,30}... | collective-permute-start | bytes 393224 | tf_op jit(solution)/shard_map/ppermute | solution.py:35
  248.6 10.9 %collective-permute-start.3 = (bf16[2,128,256]{1,2,0:T(8,128)(2,1)}, bf16[2,128,256]{1,2,0:T(8,128)(2,1)S(1)}, u32[]{:S(2)}, u32[]{:S(2)}) collective-permute-start(bf16[2,128,256]{1,2,0:T(8,128)(2,1)} %pad_maximum_fusion), channel_id=1, source_target_pairs={{0,12},{2,14},{4,16},{6,18},{8,20},{10,22},{12,24},{14,26},{16,28}... | collective-permute-start | bytes 393224 | tf_op jit(solution)/shard_map/ppermute | solution.py:35
  250.0 12.4 %collective-permute-start.4 = (bf16[2,128,256]{1,2,0:T(8,128)(2,1)}, bf16[2,128,256]{1,2,0:T(8,128)(2,1)S(1)}, u32[]{:S(2)}, u32[]{:S(2)}) collective-permute-start(bf16[2,128,256]{1,2,0:T(8,128)(2,1)} %pad_maximum_fusion), channel_id=1, source_target_pairs={{0,10},{2,12},{4,14},{6,16},{8,18},{10,20},{12,22},{14,24},{16,26}... | collective-permute-start | bytes 393224 | tf_op jit(solution)/shard_map/ppermute | solution.py:35
  251.3 12.9 %collective-permute-start.5 = (bf16[2,128,256]{1,2,0:T(8,128)(2,1)}, bf16[2,128,256]{1,2,0:T(8,128)(2,1)S(1)}, u32[]{:S(2)}, u32[]{:S(2)}) collective-permute-start(bf16[2,128,256]{1,2,0:T(8,128)(2,1)} %pad_maximum_fusion), channel_id=1, source_target_pairs={{0,8},{2,10},{4,12},{6,14},{8,16},{10,18},{12,20},{14,22},{16,24},... | collective-permute-start | bytes 393224 | tf_op jit(solution)/shard_map/ppermute | solution.py:35
  254.0 10.3 %collective-permute-start.6 = (bf16[2,128,256]{1,2,0:T(8,128)(2,1)}, bf16[2,128,256]{1,2,0:T(8,128)(2,1)S(1)}, u32[]{:S(2)}, u32[]{:S(2)}) collective-permute-start(bf16[2,128,256]{1,2,0:T(8,128)(2,1)} %pad_maximum_fusion), channel_id=1, source_target_pairs={{0,6},{2,8},{4,10},{6,12},{8,14},{10,16},{12,18},{14,20},{16,22},{... | collective-permute-start | bytes 393224 | tf_op jit(solution)/shard_map/ppermute | solution.py:35
  270.1 13.0 %collective-permute-start.12 = (bf16[256,2,256]{2,0,1:T(8,128)(2,1)S(1)}, bf16[256,2,256]{2,0,1:T(8,128)(2,1)S(1)}, u32[]{:S(2)}, u32[]{:S(2)}) collective-permute-start(bf16[256,2,256]{2,0,1:T(8,128)(2,1)S(1)} %maximum_select_fusion.1), channel_id=1, source_target_pairs={{0,16},{2,18},{4,20},{6,22},{8,24},{10,26},{12,28},{14,30},{16,0},... | collective-permute-start | bytes 786440 | tf_op jit(solution)/shard_map/ppermute | solution.py:21
  (53 other events, 237.7 us)
Sparse Core Ops, SparseCore 0:
  284.6 7.3 reduce-scatter.1
